TPU v7x, 256 devices: a whole 4x4x8 slice. The times are simulated.
256 devices in a mesh: chan: 8 (over y_hi, x), win: 32 (over y_lo, z, core).
Axes of the slice: x: 4, y: 4 (y_hi: 2, y_lo: 2; y = y_hi * 2 + y_lo), z: 8, core: 2. Of those that a mesh axis runs over, the one named last changes fastest.
Arguments:
- raw: bfloat16 [128, 3200, 1024], P('win', None, 'chan'), may hold values from -6 to 6
- offsets: int32 [128], P('win'), may hold values from 0 to 128
- quality: int32 [128, 1024], P('win', 'chan'), may hold values 0 or 1
Outputs:
- stack: bfloat16 [384, 2, 1024, 1024], P('win', None, 'chan')
All inputs are finite; a program needn't handle non-finite values. No bound on the sum of `quality` on one device may be relied on, other than what follows from the above.
Results may differ from a plain program's by a relative error of at most 0.0064.
Values may be sent and summed in bfloat16 or wider, within the bound.
A program may use at most 64 MiB of HBM per device.

v0:
```python
import math
import jax
import jax.numpy as jnp
from jax import lax
from jax.sharding import PartitionSpec as P

F = 384
L = 3072
FIRST_BIN = 60
epsilon = 1e-05


def dft_table():
    sample_idx = jnp.arange(L, dtype=jnp.int32)
    bin_idx = FIRST_BIN + jnp.arange(F, dtype=jnp.int32)
    residue = bin_idx[:, None] * sample_idx[None, :] % L
    angles = residue.astype(jnp.float32) * (2.0 * math.pi / L)
    return jnp.concatenate([jnp.cos(angles), -jnp.sin(angles)], 0).astype(jnp.bfloat16)


def cross_spectra(mine, partner):
    stack_scale = 1.0 / math.sqrt(mine.shape[0])
    real_mine = mine[:, 0]
    imag_mine = mine[:, 1]
    real_other = partner[:, 0]
    imag_other = partner[:, 1]
    real_part = jnp.einsum(
        "wfi,wfj->fij", real_mine, real_other, preferred_element_type=jnp.float32
    )
    real_part = real_part + jnp.einsum(
        "wfi,wfj->fij", imag_mine, imag_other, preferred_element_type=jnp.float32
    )
    imag_part = jnp.einsum(
        "wfi,wfj->fij", imag_mine, real_other, preferred_element_type=jnp.float32
    )
    imag_part = imag_part - jnp.einsum(
        "wfi,wfj->fij", real_mine, imag_other, preferred_element_type=jnp.float32
    )
    return (jnp.stack([real_part, imag_part], 1) * stack_scale).astype(jnp.bfloat16)


def local(raw, offsets, quality):
    table = dft_table()

    def cut_window(segment, shift_at):
        return lax.dynamic_slice_in_dim(segment, shift_at, L, 0)

    windows = jax.vmap(cut_window)(raw, offsets)
    transform = jnp.einsum("kl,wlc->wkc", table, windows, preferred_element_type=jnp.float32)
    band_power = jnp.sum(transform * transform, axis=1, keepdims=True) / F
    whiten = lax.rsqrt(band_power + epsilon) * quality.astype(jnp.float32)[:, None, :]
    block_width = raw.shape[2]
    spectra = (transform * whiten).astype(jnp.bfloat16).reshape(raw.shape[0], 2, F, block_width)
    gathered = lax.all_gather(spectra, "chan", axis=3, tiled=True)
    by_bin = lax.all_to_all(gathered, "win", split_axis=2, concat_axis=0, tiled=True)
    mine = lax.dynamic_slice_in_dim(by_bin, lax.axis_index("chan") * block_width, block_width, 3)
    return cross_spectra(mine, by_bin)


def solution(mesh):
    in_specs = (P("win", None, "chan"), P("win"), P("win", "chan"))
    out_specs = P("win", None, "chan", None)
    return jax.shard_map(local, mesh=mesh, in_specs=in_specs, out_specs=out_specs, check_vma=False)
```

profile of v0, /device:TPU:96, one launch (start us, length us, event | category | flops | bytes accessed | tf_op | source)
XLA Modules:
  0.0 393.1 jit_solution(9089974725493236142)
XLA Ops:
  6.5 0.0 all-gather.2.cloned.1.call-start
  6.5 0.7 fusion.14
  7.2 0.1 copy.21
  7.3 13.5 %while.1 = (s32[]{:T(128)}, bf16[4,3200,128]{2,1,0:T(8,128)(2,1)}, s32[4,3]{1,0:T(4,128)S(1)}, bf16[4,3072,128]{2,1,0:T(8,128)(2,1)S(1)}, s32[]{:T(128)}) while((s32[]{:T(128)}, bf16[4,3200,128]{2,1,0:T(8,128)(2,1)}, s32[4,3]{1,0:T(4,128)S(1)}, bf16[4,3072,128]{2,1,0:T(8,128)(2,1)S(1)}, s32[]{:T(128)}) %tuple.24), condition=%wide.while_cond, body=%wide.while_body.sunk | while | flops 2 | bytes 1572989 | solution.py:46
  7.3 0.7 fusion.23
  8.0 2.7 dynamic-slice_dynamic-update-slice_fusion.2
  10.7 0.7 fusion.23
  11.4 2.7 dynamic-slice_dynamic-update-slice_fusion.2
  14.1 0.7 fusion.23
  14.7 2.7 dynamic-slice_dynamic-update-slice_fusion.2
  17.5 0.7 fusion.23
  18.1 2.7 dynamic-slice_dynamic-update-slice_fusion.2
  20.8 20.3 %cosine_convert_fusion = (bf16[384,3072]{1,0:T(8,128)(2,1)S(1)}, bf16[384,3072]{1,0:T(8,128)(2,1)S(1)}) fusion(s32[384]{0:T(512)S(1)} %iota_add_fusion), kind=kLoop, calls=%fused_computation.14 | loop fusion | flops 14155776 | bytes 4720128 | tf_op jit(solution)/shard_map/convert
  41.1 0.0 copy-start.1
  41.1 2.8 multiply_reduce_fusion
  43.9 0.0 copy-done.1
  43.9 0.2 fusion.13
  44.1 0.2 reshape.12
  44.3 2.1 copy.23
  46.3 0.0 all-gather.2.cloned.1.call-update
  46.4 159.5 %all-gather.2.cloned.1.call-done = bf16[4,2,384,1024]{3,1,0,2:T(2,128)(2,1)} async-done(((bf16[4,2,384,128]{3,1,0,2:T(2,128)(2,1)}), bf16[4,2,384,1024]{3,1,0,2:T(2,128)(2,1)}) %all-gather.2.cloned.1.call-update) | async-done | bytes 6291472 | tf_op jit(solution)/shard_map/all_gather | solution.py:54
  205.9 7.5 %all-to-all-start = ((bf16[4,2,384,1024]{3,1,0,2:T(2,128)(2,1)}), bf16[4,2,384,1024]{3,1,0,2:T(2,128)(2,1)}, u32[]{:S(2)}, u32[]{:S(2)}) async-start(bf16[4,2,384,1024]{3,1,0,2:T(2,128)(2,1)} %all-gather.2.cloned.1.call-done), calls=%async_computation | async-start | bytes 12582912 | tf_op jit(solution)/shard_map/all_to_all | solution.py:55
  213.4 142.0 %all-to-all-done = bf16[4,2,384,1024]{3,1,0,2:T(2,128)(2,1)} async-done(((bf16[4,2,384,1024]{3,1,0,2:T(2,128)(2,1)}), bf16[4,2,384,1024]{3,1,0,2:T(2,128)(2,1)}, u32[]{:S(2)}, u32[]{:S(2)}) %all-to-all-start) | async-done | bytes 6291488 | tf_op jit(solution)/shard_map/all_to_all | solution.py:55
  355.4 8.8 %copy.25 = bf16[32,4,2,12,1024]{4,1,0,3,2:T(4,128)(2,1)} copy(bf16[32,4,2,12,1024]{4,2,1,3,0:T(2,128)(2,1)} %bitcast.5) | data formatting | bytes 12582912 | tf_op jit(solution)/shard_map/all_to_all | solution.py:55
  364.1 9.7 %all_to_all.16 = bf16[128,2,12,1024]{3,0,2,1:T(8,128)(2,1)} reshape(bf16[32,4,2,12,1024]{4,1,0,3,2:T(4,128)(2,1)} %copy.25) | data formatting | bytes 12582912 | tf_op jit(solution)/shard_map/all_to_all | solution.py:55
  373.8 0.0 copy-start
  373.8 3.2 fusion.10
  377.0 0.7 copy-done
  377.7 1.0 fusion.9
  378.7 1.0 add_bitcast_fusion
  379.8 1.0 subtract_bitcast_fusion
  380.8 1.9 fusion
  382.8 3.5 copy.30
  (9 shorter events, 0.1 us)
Async XLA Ops:
  6.5 199.3 %all-gather.2.cloned.1.call-start = ((), (), s32[]{:S(2)}) async-start(), calls=%async_computation.1 | async-start | bytes 7077888 | tf_op jit(solution)/shard_map/all_gather | solution.py:54
  41.1 2.8 copy-start.1
  205.9 149.5 %all-to-all-start = ((bf16[4,2,384,1024]{3,1,0,2:T(2,128)(2,1)}), bf16[4,2,384,1024]{3,1,0,2:T(2,128)(2,1)}, u32[]{:S(2)}, u32[]{:S(2)}) async-start(bf16[4,2,384,1024]{3,1,0,2:T(2,128)(2,1)} %all-gather.2.cloned.1.call-done), calls=%async_computation | async-start | bytes 12582912 | tf_op jit(solution)/shard_map/all_to_all | solution.py:55
  373.8 3.9 copy-start
Sparse Core Ops, SparseCore 0:
  46.5 159.3 all-gather.1
where the time goes:
time: 394 us; the launch traced here: 393 us
  waiting for transfers between devices  301 us (76%)
  local copies, waits for them, and re-layouts  38.4 us (10%)
  other arithmetic  23 us (6%)
  between operations  13.5 us (3%)
  matrix products  9.09 us (2%)
  starting transfers between devices  7.54 us (2%)
    all_gather x1, waiting for transfers between devices, local(): gathered = lax.all_gather(spectra, 'chan', axis=3, tiled=True)  159 us
    all_to_all x1, waiting for transfers between devices, local(): lax.all_to_all(gathered, 'win', split_axis=2, concat_axis=0, tiled=True)  142 us
    another operation x1, other arithmetic  20.3 us
    all_to_all x2, local copies, waits for them, and re-layouts, local(): lax.all_to_all(gathered, 'win', split_axis=2, concat_axis=0, tiled=True)  18.4 us
    gather x12, local copies, waits for them, and re-layouts  13.4 us
  transfers between devices with their start and end apart: 2, of which 2 were waited for; matrix products, arithmetic and copies ran while one was open for 0% of the time, Pallas kernels for 0%

commit v1 on v0

--- a/solution.py
+++ b/solution.py
@@ -51,7 +51,9 @@
     whiten = lax.rsqrt(band_power + epsilon) * quality.astype(jnp.float32)[:, None, :]
     block_width = raw.shape[2]
     spectra = (transform * whiten).astype(jnp.bfloat16).reshape(raw.shape[0], 2, F, block_width)
-    gathered = lax.all_gather(spectra, "chan", axis=3, tiled=True)
+    gathered = jnp.concatenate(
+        lax.all_to_all(jnp.stack([spectra] * lax.axis_size("chan")), "chan", 0, 0), axis=3
+    )
     by_bin = lax.all_to_all(gathered, "win", split_axis=2, concat_axis=0, tiled=True)
     mine = lax.dynamic_slice_in_dim(by_bin, lax.axis_index("chan") * block_width, block_width, 3)
     return cross_spectra(mine, by_bin)

time: 394 us -> 321 us (0.81)
  waiting for transfers between devices: 301 us -> 142 us
  blocking collectives: 0 us -> 80.7 us
  local copies, waits for them, and re-layouts: 38.4 us -> 56.5 us
  between operations: 13.5 us -> 0.11 us
    all_gather x1 -> x0, waiting for transfers between devices: 159 us -> none  [local(): gathered = lax.all_gather(spectra, 'chan', axis=3, tiled=True)]
    all_to_all x0 -> x1, blocking collectives: none -> 80.7 us  [local(): lax.all_to_all(jnp.stack([spectra] * lax.axis_size('chan')), 'chan', 0, 0)]
    reshape x2 -> x1, local copies, waits for them, and re-layouts: 2.27 us -> 16.2 us  [local(): jnp.concatenate(lax.all_to_all(jnp.stack([spectra] * lax.axis_size('chan'...]
  transfers between devices with their start and end apart: 2 -> 1, of which waited for: 2 -> 1; matrix products, arithmetic and copies ran while one was open for 0% -> 0% of each run, Pallas kernels for 0% -> 0%
where the time goes in v1:
time: 321 us; the launch traced here: 319 us
  waiting for transfers between devices  142 us (44%)
  blocking collectives  80.7 us (25%)
  local copies, waits for them, and re-layouts  56.5 us (18%)
  other arithmetic  23 us (7%)
  matrix products  9.09 us (3%)
  starting transfers between devices  7.99 us (2%)
    all_to_all x1, waiting for transfers between devices, local(): lax.all_to_all(gathered, 'win', split_axis=2, concat_axis=0, tiled=True)  142 us
    all_to_all x1, blocking collectives, local(): lax.all_to_all(jnp.stack([spectra] * lax.axis_size('chan')), 'chan', 0, 0)  80.7 us
    another operation x1, other arithmetic  20.3 us
    all_to_all x2, local copies, waits for them, and re-layouts, local(): lax.all_to_all(gathered, 'win', split_axis=2, concat_axis=0, tiled=True)  18.4 us
    reshape x1, local copies, waits for them, and re-layouts, local(): jnp.concatenate(lax.all_to_all(jnp.stack([spectra] * lax.axis_size('chan'...  16.2 us
    gather x12, local copies, waits for them, and re-layouts  13 us
    all_to_all x1, starting transfers between devices, local(): lax.all_to_all(gathered, 'win', split_axis=2, concat_axis=0, tiled=True)  7.99 us
  transfers between devices with their start and end apart: 1, of which 1 were waited for; matrix products, arithmetic and copies ran while one was open for 0% of the time, Pallas kernels for 0%

profile of v1, /device:TPU:96, one launch (start us, length us, event | category | flops | bytes accessed | tf_op | source)
XLA Modules:
  0.0 319.4 jit_solution(11465223586393775873)
XLA Ops:
  0.0 0.7 fusion.13
  0.7 0.1 copy.22
  0.8 13.0 %while.1 = (s32[]{:T(128)}, bf16[4,3200,128]{2,1,0:T(8,128)(2,1)}, s32[4,3]{1,0:T(4,128)S(1)}, bf16[4,3072,128]{2,1,0:T(8,128)(2,1)S(1)}, s32[]{:T(128)}) while((s32[]{:T(128)}, bf16[4,3200,128]{2,1,0:T(8,128)(2,1)}, s32[4,3]{1,0:T(4,128)S(1)}, bf16[4,3072,128]{2,1,0:T(8,128)(2,1)S(1)}, s32[]{:T(128)}) %tuple.24), condition=%wide.while_cond, body=%wide.while_body.sunk | while | flops 2 | bytes 1572989 | solution.py:46
  0.8 0.6 fusion.22
  1.4 2.6 dynamic-slice_dynamic-update-slice_fusion.2
  4.0 0.6 fusion.22
  4.6 2.6 dynamic-slice_dynamic-update-slice_fusion.2
  7.3 0.6 fusion.22
  7.9 2.6 dynamic-slice_dynamic-update-slice_fusion.2
  10.6 0.6 fusion.22
  11.2 2.6 dynamic-slice_dynamic-update-slice_fusion.2
  13.8 20.3 %cosine_convert_fusion = (bf16[384,3072]{1,0:T(8,128)(2,1)S(1)}, bf16[384,3072]{1,0:T(8,128)(2,1)S(1)}) fusion(s32[384]{0:T(512)S(1)} %iota_add_fusion), kind=kLoop, calls=%fused_computation.14 | loop fusion | flops 14155776 | bytes 4720128 | tf_op jit(solution)/shard_map/convert
  34.1 0.0 copy-start.1
  34.1 2.8 multiply_reduce_fusion
  36.9 0.0 copy-done.1
  36.9 0.2 multiply_convert_fusion
  37.1 0.1 copy.42
  37.2 1.0 stack.12
  38.2 80.7 %all_to_all.23 = bf16[8,4,2,384,128]{3,4,2,1,0:T(8,128)(2,1)S(1)} all-to-all(bf16[8,4,2,384,128]{3,4,2,1,0:T(8,128)(2,1)S(1)} %stack.12), channel_id=1, replica_groups=mesh['chan'=8,'win'=32] {'chan'}, dimensions={0} | all-to-all | bytes 12582912 | tf_op jit(solution)/shard_map/all_to_all | solution.py:55
  118.8 3.6 %copy.25 = bf16[8,4,2,384,128]{3,4,0,2,1:T(8,128)(2,1)} copy(bf16[8,4,2,384,128]{3,4,2,1,0:T(8,128)(2,1)S(1)} %all_to_all.23) | data formatting | bytes 12582912 | tf_op jit(solution)/shard_map/all_to_all | solution.py:55
  122.4 16.2 %copy.26 = bf16[4,2,384,1024]{3,1,0,2:T(2,128)(2,1)} copy(bf16[4,2,384,1024]{2,3,1,0:T(8,128)(2,1)} %bitcast.51) | data formatting | bytes 12582912 | tf_op jit(solution)/shard_map/reshape | solution.py:54
  138.6 8.0 %all-to-all-start.1 = ((bf16[4,2,384,1024]{3,1,0,2:T(2,128)(2,1)}), bf16[4,2,384,1024]{3,1,0,2:T(2,128)(2,1)}, u32[]{:S(2)}, u32[]{:S(2)}) async-start(bf16[4,2,384,1024]{3,1,0,2:T(2,128)(2,1)} %copy.26), calls=%async_computation.1 | async-start | bytes 12582912 | tf_op jit(solution)/shard_map/all_to_all | solution.py:57
  146.6 142.0 %all-to-all-done.1 = bf16[4,2,384,1024]{3,1,0,2:T(2,128)(2,1)} async-done(((bf16[4,2,384,1024]{3,1,0,2:T(2,128)(2,1)}), bf16[4,2,384,1024]{3,1,0,2:T(2,128)(2,1)}, u32[]{:S(2)}, u32[]{:S(2)}) %all-to-all-start.1) | async-done | bytes 6291488 | tf_op jit(solution)/shard_map/all_to_all | solution.py:57
  288.6 8.8 %copy.28 = bf16[32,4,2,12,1024]{4,1,0,3,2:T(4,128)(2,1)} copy(bf16[32,4,2,12,1024]{4,2,1,3,0:T(2,128)(2,1)} %bitcast.7) | data formatting | bytes 12582912 | tf_op jit(solution)/shard_map/all_to_all | solution.py:57
  297.3 9.7 %all_to_all.20 = bf16[128,2,12,1024]{3,0,2,1:T(8,128)(2,1)} reshape(bf16[32,4,2,12,1024]{4,1,0,3,2:T(4,128)(2,1)} %copy.28) | data formatting | bytes 12582912 | tf_op jit(solution)/shard_map/all_to_all | solution.py:57
  307.0 0.0 copy-start
  307.0 3.2 fusion.10
  310.2 0.7 copy-done
  310.9 1.0 fusion.9
  311.9 1.0 add_bitcast_fusion
  312.9 1.0 subtract_bitcast_fusion
  314.0 1.9 fusion
  315.9 3.5 %copy.33 = bf16[12,2,128,1024]{3,2,1,0:T(8,128)(2,1)} copy(bf16[12,2,128,1024]{3,2,0,1:T(8,128)(2,1)S(1)} %fusion) | data formatting | bytes 12582912 | tf_op jit(solution)/shard_map/convert_element_type | solution.py:39
  (9 shorter events, 0.1 us)
Async XLA Ops:
  34.1 2.8 copy-start.1
  138.6 150.0 %all-to-all-start.1 = ((bf16[4,2,384,1024]{3,1,0,2:T(2,128)(2,1)}), bf16[4,2,384,1024]{3,1,0,2:T(2,128)(2,1)}, u32[]{:S(2)}, u32[]{:S(2)}) async-start(bf16[4,2,384,1024]{3,1,0,2:T(2,128)(2,1)} %copy.26), calls=%async_computation.1 | async-start | bytes 12582912 | tf_op jit(solution)/shard_map/all_to_all | solution.py:57
  307.0 3.9 %copy-start = (bf16[128,2,12,1024]{3,0,2,1:T(8,128)(2,1)S(1)}, bf16[128,2,12,1024]{3,0,2,1:T(8,128)(2,1)}, u32[]{:S(2)}) copy-start(bf16[128,2,12,1024]{3,0,2,1:T(8,128)(2,1)} %all_to_all.20) | copy-start | bytes 18874372
